TPU v7x, 256 devices: a whole 4x4x8 slice. The times are simulated.
256 devices in a mesh: band: 8 (over y_hi, x), item: 32 (over y_lo, z, core).
Axes of the slice: x: 4, y: 4 (y_hi: 2, y_lo: 2; y = y_hi * 2 + y_lo), z: 8, core: 2. Of those that a mesh axis runs over, the one named last changes fastest.
Arguments:
- ratings: bfloat16 [49152, 16384], P('band', 'item'), may hold values from -6 to 6
- rating_mask: int32 [384, 16384], P('band', 'item'), may hold values 0 or 1
- attributes: bfloat16 [24576, 16384], P('band', 'item'), may hold values from -6 to 6
- attribute_mask: int32 [192, 16384], P('band', 'item'), may hold values 0 or 1
- user_factors: bfloat16 [49152, 256], P('band', 'item'), as said below
- tag_factors: bfloat16 [24576, 256], P('band', 'item'), as said below
Outputs:
- item_factors: float32 [16384, 256], P('item')
Inputs may be any that keep to these rules, and one draw needn't show every extreme that they name: `user_factors`: user factors of order one over the square root of 49152. `tag_factors`: tag factors of order one over the square root of 24576.
All inputs are finite; a program needn't handle non-finite values. No bound on the sum of `rating_mask` or of `attribute_mask` on one device may be relied on, other than what follows from the above.
Results may differ from a plain program's by a relative error of at most 0.0003.
Values may be sent and summed in bfloat16 or wider, within the bound.
No kernel may reach another device: no remote copies, remote signals or barrier semaphores. Data moves between devices by JAX's collectives and lax.ppermute only.
A program may use at most 64 MiB of HBM per device.

v0:
```python
import jax
import jax.numpy as jnp
from jax import lax
from jax.sharding import PartitionSpec as P

LAMBDA = 0.5
REG = 0.1


def apply_mask(values, mask):
    rows, cols = values.shape
    blocks = mask.shape[0]
    shaped = values.reshape(blocks, rows // blocks, cols) * mask.astype(values.dtype)[:, None, :]
    return shaped.reshape(rows, cols)


def inner(left, right):
    return lax.dot_general(
        left, right, (((0,), (0,)), ((), ())), preferred_element_type=jnp.float32
    )


def solve_rows(factor, rhs):
    half = lax.linalg.triangular_solve(factor, rhs, left_side=False, lower=True, transpose_a=True)
    return lax.linalg.triangular_solve(factor, half, left_side=False, lower=True, transpose_a=False)


def band_gram(partial_gram):
    return lax.psum(partial_gram, "band")


def finish_gram(summed_gram, rank):
    return jnp.linalg.cholesky(summed_gram + REG * jnp.eye(rank, dtype=jnp.float32))


def body(ratings, rating_mask, attributes, attribute_mask, user_factors, tag_factors):
    users = lax.all_gather(user_factors, "item", axis=1, tiled=True)
    tags = lax.all_gather(tag_factors, "item", axis=1, tiled=True)
    rank = users.shape[1]
    partial_gram = inner(users, users) + LAMBDA * inner(tags, tags)
    masked_ratings = apply_mask(ratings, rating_mask)
    masked_attributes = apply_mask(attributes, attribute_mask)
    local_rhs = inner(masked_ratings, users) + LAMBDA * inner(masked_attributes, tags)
    summed_gram = band_gram(partial_gram)
    summed_rhs = lax.psum(local_rhs, "band")
    factor = finish_gram(summed_gram, rank)
    return solve_rows(factor, summed_rhs)


def solution(mesh):
    in_specs = (
        P("band", "item"),
        P("band", "item"),
        P("band", "item"),
        P("band", "item"),
        P("band", "item"),
        P("band", "item"),
    )
    out_specs = P("item", None)
    return jax.shard_map(body, mesh=mesh, in_specs=in_specs, out_specs=out_specs, check_vma=False)
```

profile of v0, /device:TPU:32, one launch (start us, length us, event | category | flops | bytes accessed | tf_op | source)
XLA Modules:
  0.0 317.1 jit_solution(6339761031712931756)
XLA Ops:
  6.5 0.0 all-gather.5.cloned.1.call-start
  6.5 0.7 all-gather.5.cloned.1.call-update
  7.3 0.0 all-gather.3.cloned.1.call-start
  7.3 0.7 all-gather.3.cloned.1.call-update
  8.0 0.0 all-reduce.4.cloned.1.call-start
  8.1 0.8 convert_element_type.8
  8.9 0.9 convert_element_type.7
  9.8 0.0 copy-start
  9.8 2.3 bitcast_multiply_fusion.1
  12.0 1.5 copy-done
  13.5 3.1 bitcast_multiply_fusion
  16.6 58.8 %all-gather.5.cloned.1.call-done = bf16[3072,256]{0,1:T(8,128)(2,1)} async-done(((bf16[3072,8]{0,1:T(8,128)(2,1)}), bf16[3072,256]{0,1:T(8,128)(2,1)}) %all-gather.5.cloned.1.call-update) | async-done | bytes 1572880 | tf_op jit(solution)/shard_map/all_gather | solution.py:38
  75.4 3.2 %convolution_multiply_fusion = f32[512,256]{1,0:T(8,128)} fusion(bf16[3072,512]{1,0:T(8,128)(2,1)S(1)} %bitcast_multiply_fusion.1, bf16[3072,256]{0,1:T(8,128)(2,1)} %all-gather.5.cloned.1.call-done), kind=kOutput, calls=%fused_computation.4 | convolution fusion | flops 805437440 | bytes 5242880 | tf_op jit(solution)/shard_map/dot_general | solution.py:18
  78.6 0.0 copy-start.2
  78.6 64.3 %all-gather.3.cloned.1.call-done = bf16[6144,256]{0,1:T(8,128)(2,1)} async-done(((bf16[6144,8]{0,1:T(8,128)(2,1)}), bf16[6144,256]{0,1:T(8,128)(2,1)}) %all-gather.3.cloned.1.call-update) | async-done | bytes 3145744 | tf_op jit(solution)/shard_map/all_gather | solution.py:37
  142.9 0.0 copy-start.1
  142.9 4.0 %fusion.13 = f32[256,256]{1,0:T(8,128)S(1)} fusion(bf16[6144,256]{0,1:T(8,128)(2,1)} %all-gather.3.cloned.1.call-done), kind=kOutput, calls=%fused_computation.41 | convolution fusion | flops 805306368 | bytes 3407872 | tf_op jit(solution)/shard_map/dot_general | solution.py:18
  146.9 0.0 copy-done.2
  146.9 0.0 copy-start.4
  146.9 1.3 fusion
  148.2 0.0 copy-done.1
  148.2 0.0 copy-done.4
  148.2 4.5 %convolution_add_fusion = f32[512,256]{1,0:T(8,128)} fusion(f32[512,256]{1,0:T(8,128)S(1)} %copy-done.4, bf16[6144,512]{1,0:T(8,128)(2,1)S(1)} %copy-done.1, bf16[6144,256]{0,1:T(8,128)(2,1)} %all-gather.3.cloned.1.call-done), kind=kOutput, calls=%fused_computation.5 | convolution fusion | flops 1610743808 | bytes 10485760 | tf_op jit(solution)/shard_map/dot_general | solution.py:18
  152.8 0.0 all-reduce.4.cloned.1.call-update
  152.8 92.3 %all-reduce.4.cloned.1.call-done = (f32[512,256]{1,0:T(8,128)}, f32[256,256]{1,0:T(8,128)}) async-done(((f32[512,256]{1,0:T(8,128)}, f32[256,256]{1,0:T(8,128)}), (f32[512,256]{1,0:T(8,128)}, f32[256,256]{1,0:T(8,128)})) %all-reduce.4.cloned.1.call-update) | async-done | bytes 786448 | tf_op jit(solution)/shard_map/psum | solution.py:45
  245.1 0.0 copy-start.3
  245.1 1.0 select_add_fusion
  246.2 0.1 copy.7
  246.3 1.0 fusion.3
  247.3 11.7 %cholesky.49 = f32[128,128]{1,0:T(8,128)S(1)} custom-call(f32[128,128]{1,0:T(8,128)S(1)} %cholesky.115), custom_call_target="Cholesky" | custom-call | tf_op jit(solution)/shard_map/jit(cholesky)/cholesky | solution.py:33
  259.1 9.8 %custom-call.16 = f32[1,128,128]{1,2,0:T(8,128)S(1)} custom-call(f32[1,128,128]{2,1,0:T(8,128)S(1)} %get-tuple-element.28), custom_call_target="InvertDiagBlocksLowerTriangular" | custom-call | tf_op jit(solution)/shard_map/jit(cholesky)/cholesky | solution.py:33
  268.9 0.2 constant_dynamic-update-slice_fusion.1
  269.1 0.3 convolution_subtract_fusion.2
  269.4 11.9 %cholesky.103 = f32[128,128]{1,0:T(8,128)S(1)} custom-call(f32[128,128]{1,0:T(8,128)S(1)} %convolution_subtract_fusion.2), custom_call_target="Cholesky" | custom-call | tf_op jit(solution)/shard_map/jit(cholesky)/cholesky | solution.py:33
  281.3 0.7 compare_reduce_fusion
  283.3 0.1 triangular_solve.70
  283.3 3.9 %while.1 = (s32[]{:T(128)}, f32[256,256]{1,0:T(8,128)S(1)}, s32[2,2]{1,0:T(2,128)S(1)}, f32[2,128,128]{2,1,0:T(8,128)S(1)}, s32[]{:T(128)}) while((s32[]{:T(128)}, f32[256,256]{1,0:T(8,128)S(1)}, s32[2,2]{1,0:T(2,128)S(1)}, f32[2,128,128]{2,1,0:T(8,128)S(1)}, s32[]{:T(128)}) %tuple.23), condition=%wide.while_cond, body=%wide.while_body.sunk | while | flops 2 | bytes 131189 | solution.py:24
  283.4 0.6 fusion.30
  283.9 1.4 bitcast_dynamic-update-slice_fusion.2
  285.3 0.6 fusion.30
  285.9 1.4 bitcast_dynamic-update-slice_fusion.2
  287.3 19.7 %custom-call.17 = f32[2,128,128]{1,2,0:T(8,128)S(1)} custom-call(f32[2,128,128]{2,1,0:T(8,128)S(1)} %get-tuple-element.12), custom_call_target="InvertDiagBlocksLowerTriangular" | custom-call | tf_op jit(solution)/shard_map/triangular_solve | solution.py:24
  307.0 0.0 copy-done.3
  307.0 0.4 fusion.1
  307.4 0.4 convolution_subtract_fusion.1
  307.7 0.4 fusion.9
  308.1 0.4 fusion.8
  308.5 0.6 convolution_subtract_fusion
  309.1 0.4 fusion.7
  309.6 1.0 copy.8
  (10 shorter events, 0.2 us)
Async XLA Ops:
  6.5 68.9 %all-gather.5.cloned.1.call-start = ((), (), s32[]{:S(2)}) async-start(), calls=%async_computation.1 | async-start | bytes 1622016 | tf_op jit(solution)/shard_map/all_gather | solution.py:38
  7.3 135.6 %all-gather.3.cloned.1.call-start = ((), (), s32[]{:S(2)}) async-start(), calls=%async_computation | async-start | bytes 3244032 | tf_op jit(solution)/shard_map/all_gather | solution.py:37
  8.0 237.1 %all-reduce.4.cloned.1.call-start = ((), (), s32[]{:S(2)}) async-start(), calls=%async_computation.2 | async-start | bytes 1572864 | tf_op jit(solution)/shard_map/psum | solution.py:45
  9.8 3.7 %copy-start = (bf16[6144,512]{1,0:T(8,128)(2,1)S(1)}, bf16[6144,512]{1,0:T(8,128)(2,1)}, u32[]{:S(2)}) copy-start(bf16[6144,512]{1,0:T(8,128)(2,1)} %param.6) | copy-start | bytes 18874372
  78.6 68.3 %copy-start.2 = (bf16[3072,256]{0,1:T(8,128)(2,1)S(1)}, bf16[3072,256]{0,1:T(8,128)(2,1)}, u32[]{:S(2)}) copy-start(bf16[3072,256]{0,1:T(8,128)(2,1)} %all-gather.5.cloned.1.call-done) | copy-start | bytes 4718596
  142.9 5.3 %copy-start.1 = (bf16[6144,512]{1,0:T(8,128)(2,1)S(1)}, bf16[6144,512]{1,0:T(8,128)(2,1)}, u32[]{:S(2)}) copy-start(bf16[6144,512]{1,0:T(8,128)(2,1)} %bitcast_multiply_fusion) | copy-start | bytes 18874372
  146.9 1.3 copy-start.4
  245.1 61.8 %copy-start.3 = (f32[512,256]{1,0:T(8,128)S(1)}, f32[512,256]{1,0:T(8,128)}, u32[]{:S(2)}) copy-start(f32[512,256]{1,0:T(8,128)} %get-tuple-element.21) | copy-start | bytes 1572868
Sparse Core Ops, SparseCore 0:
  9.2 66.1 all-gather.4
  77.3 65.5 all-gather.2
  152.9 92.1 all-reduce.3
where the time goes:
time: 317 us
  waiting for transfers between devices  217 us (68%)
  other arithmetic  63 us (20%)
  matrix products  16 us (5%)
  between operations  14.6 us (5%)
  local copies, waits for them, and re-layouts  6.6 us (2%)
    psum x1, waiting for transfers between devices, body(): summed_rhs = lax.psum(local_rhs, 'band')  92.3 us
    all_gather x1, waiting for transfers between devices, body(): users = lax.all_gather(user_factors, 'item', axis=1, tiled=True)  64.3 us
    all_gather x1, waiting for transfers between devices, body(): tags = lax.all_gather(tag_factors, 'item', axis=1, tiled=True)  58.8 us
    another operation x6, other arithmetic, finish_gram(): jnp.linalg.cholesky(summed_gram + REG * jnp.eye(rank, dtype=jnp.float32))  34.1 us
    another operation x3, other arithmetic, solve_rows(): lax.linalg.triangular_solve(factor, rhs, left_side=False, lower=True, tra...  19.7 us
    dot_general x4, matrix products, inner(): lax.dot_general(left, right, (((0,), (0,)), ((), ())), preferred_element_...  13 us
  transfers between devices with their start and end apart: 3, of which 3 were waited for; matrix products, arithmetic and copies ran while one was open for 3% of the time, Pallas kernels for 0%

commit v1 on v0

--- a/solution.py
+++ b/solution.py
@@ -42,7 +42,7 @@
     masked_attributes = apply_mask(attributes, attribute_mask)
     local_rhs = inner(masked_ratings, users) + LAMBDA * inner(masked_attributes, tags)
     summed_gram = band_gram(partial_gram)
-    summed_rhs = lax.psum(local_rhs, "band")
+    summed_rhs = jnp.sum(lax.all_gather(local_rhs, "band"), axis=0)
     factor = finish_gram(summed_gram, rank)
     return solve_rows(factor, summed_rhs)
 

time: 317 us -> 331 us (1.044)
  waiting for transfers between devices: 217 us -> 224 us
    all_gather x0 -> x1, waiting for transfers between devices: none -> 16.3 us  [body(): summed_rhs = jnp.sum(lax.all_gather(local_rhs, 'band'), axis=0)]
    psum x1, waiting for transfers between devices: 92.3 us -> 83.6 us  [band_gram(): return lax.psum(partial_gram, 'band')]
  transfers between devices with their start and end apart: 3 -> 4, of which waited for: 3 -> 4; matrix products, arithmetic and copies ran while one was open for 3% -> 23% of each run, Pallas kernels for 0% -> 0%
where the time goes in v1:
time: 331 us; the launch traced here: 329 us
  waiting for transfers between devices  224 us (68%)
  other arithmetic  65.3 us (20%)
  matrix products  17.7 us (5%)
  between operations  14.6 us (4%)
  local copies, waits for them, and re-layouts  6.76 us (2%)
    psum x1, waiting for transfers between devices, band_gram(): return lax.psum(partial_gram, 'band')  83.6 us
    all_gather x1, waiting for transfers between devices, body(): users = lax.all_gather(user_factors, 'item', axis=1, tiled=True)  64.3 us
    all_gather x1, waiting for transfers between devices, body(): tags = lax.all_gather(tag_factors, 'item', axis=1, tiled=True)  58.8 us
    another operation x6, other arithmetic, finish_gram(): jnp.linalg.cholesky(summed_gram + REG * jnp.eye(rank, dtype=jnp.float32))  34 us
    another operation x3, other arithmetic, solve_rows(): lax.linalg.triangular_solve(factor, rhs, left_side=False, lower=True, tra...  19.7 us
    all_gather x1, waiting for transfers between devices, body(): summed_rhs = jnp.sum(lax.all_gather(local_rhs, 'band'), axis=0)  16.3 us
    dot_general x4, matrix products, inner(): lax.dot_general(left, right, (((0,), (0,)), ((), ())), preferred_element_...  14.7 us
  transfers between devices with their start and end apart: 4, of which 4 were waited for; matrix products, arithmetic and copies ran while one was open for 23% of the time, Pallas kernels for 0%

profile of v1, /device:TPU:32, one launch (start us, length us, event | category | flops | bytes accessed | tf_op | source)
XLA Modules:
  0.0 329.3 jit_solution(9320819123209657083)
XLA Ops:
  6.5 0.0 all-gather.7.cloned.1.call-start
  6.5 0.7 all-gather.7.cloned.1.call-update
  7.3 0.0 all-gather.5.cloned.1.call-start
  7.3 0.7 all-gather.5.cloned.1.call-update
  8.0 0.0 all-reduce.3.cloned.1.call-start
  8.1 0.8 convert_element_type.8
  8.9 0.9 convert_element_type.7
  9.8 0.0 copy-start
  9.8 2.3 bitcast_multiply_fusion.1
  12.0 1.5 copy-done
  13.5 3.1 bitcast_multiply_fusion
  16.6 58.8 %all-gather.7.cloned.1.call-done = bf16[3072,256]{0,1:T(8,128)(2,1)} async-done(((bf16[3072,8]{0,1:T(8,128)(2,1)}), bf16[3072,256]{0,1:T(8,128)(2,1)}) %all-gather.7.cloned.1.call-update) | async-done | bytes 1572880 | tf_op jit(solution)/shard_map/all_gather | solution.py:38
  75.4 3.2 convolution_multiply_fusion
  78.6 0.0 copy-start.1
  78.6 64.3 %all-gather.5.cloned.1.call-done = bf16[6144,256]{0,1:T(8,128)(2,1)} async-done(((bf16[6144,8]{0,1:T(8,128)(2,1)}), bf16[6144,256]{0,1:T(8,128)(2,1)}) %all-gather.5.cloned.1.call-update) | async-done | bytes 3145744 | tf_op jit(solution)/shard_map/all_gather | solution.py:37
  142.9 3.9 %fusion.13 = f32[256,256]{1,0:T(8,128)S(1)} fusion(bf16[6144,256]{0,1:T(8,128)(2,1)} %all-gather.5.cloned.1.call-done), kind=kOutput, calls=%fused_computation.41 | convolution fusion | flops 805306368 | bytes 3407872 | tf_op jit(solution)/shard_map/dot_general | solution.py:18
  146.8 0.0 copy-done.1
  146.8 0.0 copy-start.2
  146.8 1.3 fusion
  148.1 0.0 all-reduce.3.cloned.1.call-update
  148.1 0.2 all-gather.9.cloned.1.call-start
  148.3 0.0 copy-done.2
  148.4 6.3 %convolution_add_fusion = f32[512,256]{1,0:T(8,128)} fusion(f32[512,256]{1,0:T(8,128)S(1)} %copy-done.2, bf16[6144,512]{1,0:T(8,128)(2,1)} %bitcast_multiply_fusion, bf16[6144,256]{0,1:T(8,128)(2,1)} %all-gather.5.cloned.1.call-done), kind=kOutput, calls=%fused_computation.5 | convolution fusion | flops 1610743808 | bytes 10485760 | tf_op jit(solution)/shard_map/dot_general | solution.py:18
  154.7 0.0 all-gather.9.cloned.1.call-update
  154.7 83.6 %all-reduce.3.cloned.1.call-done = f32[256,256]{1,0:T(8,128)} async-done(((f32[256,256]{1,0:T(8,128)}), f32[256,256]{1,0:T(8,128)}) %all-reduce.3.cloned.1.call-update) | async-done | bytes 262160 | tf_op jit(solution)/shard_map/psum | solution.py:29
  238.3 1.0 select_add_fusion
  239.3 0.1 copy.7
  239.5 1.0 fusion.3
  240.5 11.7 %cholesky.49 = f32[128,128]{1,0:T(8,128)S(1)} custom-call(f32[128,128]{1,0:T(8,128)S(1)} %cholesky.115), custom_call_target="Cholesky" | custom-call | tf_op jit(solution)/shard_map/jit(cholesky)/cholesky | solution.py:33
  252.2 9.8 %custom-call.16 = f32[1,128,128]{1,2,0:T(8,128)S(1)} custom-call(f32[1,128,128]{2,1,0:T(8,128)S(1)} %get-tuple-element.26), custom_call_target="InvertDiagBlocksLowerTriangular" | custom-call | tf_op jit(solution)/shard_map/jit(cholesky)/cholesky | solution.py:33
  262.1 0.2 constant_dynamic-update-slice_fusion.1
  262.3 0.3 convolution_subtract_fusion.2
  262.5 11.7 %cholesky.103 = f32[128,128]{1,0:T(8,128)S(1)} custom-call(f32[128,128]{1,0:T(8,128)S(1)} %convolution_subtract_fusion.2), custom_call_target="Cholesky" | custom-call | tf_op jit(solution)/shard_map/jit(cholesky)/cholesky | solution.py:33
  274.3 0.7 compare_reduce_fusion
  276.3 0.1 triangular_solve.70
  276.4 4.3 %while.1 = (s32[]{:T(128)}, f32[256,256]{1,0:T(8,128)S(1)}, s32[2,2]{1,0:T(2,128)S(1)}, f32[2,128,128]{2,1,0:T(8,128)S(1)}, s32[]{:T(128)}) while((s32[]{:T(128)}, f32[256,256]{1,0:T(8,128)S(1)}, s32[2,2]{1,0:T(2,128)S(1)}, f32[2,128,128]{2,1,0:T(8,128)S(1)}, s32[]{:T(128)}) %tuple.23), condition=%wide.while_cond, body=%wide.while_body.sunk | while | flops 2 | bytes 131189 | solution.py:24
  276.6 0.6 fusion.30
  277.2 1.4 bitcast_dynamic-update-slice_fusion.2
  278.6 0.6 fusion.30
  279.3 1.4 bitcast_dynamic-update-slice_fusion.2
  280.7 19.7 %custom-call.17 = f32[2,128,128]{1,2,0:T(8,128)S(1)} custom-call(f32[2,128,128]{2,1,0:T(8,128)S(1)} %get-tuple-element.12), custom_call_target="InvertDiagBlocksLowerTriangular" | custom-call | tf_op jit(solution)/shard_map/triangular_solve | solution.py:24
  300.4 16.3 %all-gather.9.cloned.1.call-done = f32[4096,256]{1,0:T(8,128)} async-done(((f32[512,256]{1,0:T(8,128)}), f32[4096,256]{1,0:T(8,128)}) %all-gather.9.cloned.1.call-update) | async-done | bytes 4194320 | tf_op jit(solution)/shard_map/all_gather | solution.py:45
  316.7 2.5 reduce_sum.9
  319.2 0.4 fusion.1
  319.6 0.4 convolution_subtract_fusion.1
  320.0 0.4 fusion.9
  320.4 0.4 fusion.8
  320.7 0.6 convolution_subtract_fusion
  321.3 0.4 fusion.7
  321.8 1.0 copy.8
  (10 shorter events, 0.2 us)
Async XLA Ops:
  6.5 68.9 %all-gather.7.cloned.1.call-start = ((), (), s32[]{:S(2)}) async-start(), calls=%async_computation.1 | async-start | bytes 1622016 | tf_op jit(solution)/shard_map/all_gather | solution.py:38
  7.3 135.6 %all-gather.5.cloned.1.call-start = ((), (), s32[]{:S(2)}) async-start(), calls=%async_computation | async-start | bytes 3244032 | tf_op jit(solution)/shard_map/all_gather | solution.py:37
  8.0 230.3 %all-reduce.3.cloned.1.call-start = ((), (), s32[]{:S(2)}) async-start(), calls=%async_computation.2 | async-start | bytes 524288 | tf_op jit(solution)/shard_map/psum | solution.py:29
  9.8 3.7 %copy-start = (bf16[6144,512]{1,0:T(8,128)(2,1)S(1)}, bf16[6144,512]{1,0:T(8,128)(2,1)}, u32[]{:S(2)}) copy-start(bf16[6144,512]{1,0:T(8,128)(2,1)} %param.6) | copy-start | bytes 18874372
  78.6 68.1 %copy-start.1 = (bf16[3072,256]{0,1:T(8,128)(2,1)S(1)}, bf16[3072,256]{0,1:T(8,128)(2,1)}, u32[]{:S(2)}) copy-start(bf16[3072,256]{0,1:T(8,128)(2,1)} %all-gather.7.cloned.1.call-done) | copy-start | bytes 4718596
  146.8 1.6 copy-start.2
  148.1 168.6 %all-gather.9.cloned.1.call-start = ((), (), s32[]{:S(2)}) async-start(), calls=%async_computation.3 | async-start | bytes 4718592 | tf_op jit(solution)/shard_map/all_gather | solution.py:45
Sparse Core Ops, SparseCore 0:
  9.2 66.1 all-gather.6
  77.3 65.5 all-gather.4
  148.2 90.0 all-reduce.2
  241.2 75.4 all-gather.8
